TPU v7x, 32 devices: a whole 2x2x4 slice. The times are simulated.
32 devices in a mesh: grp: 8 (over z, y), chan: 4 (over x, core).
Axes of the slice: x: 2, y: 2, z: 4, core: 2. Of those that a mesh axis runs over, the one named last changes fastest.
Arguments:
- grad_out: bfloat16 [64, 8, 16, 128], P('grp', 'chan'), may hold values from -6 to 6
- feat_full: bfloat16 [64, 8, 16, 128], P('grp', 'chan'), may hold values from -6 to 6
- filters_full: bfloat16 [3, 3, 3, 128, 128], replicated, may hold values from -0.109375 to 0.109375
- upsample_weight: bfloat16 [2, 2, 2, 512, 128], replicated, may hold values from -0.1875 to 0.1875
- filters_half: bfloat16 [3, 3, 3, 512, 512], P(None, None, None, None, 'chan'), may hold values from -0.0546875 to 0.0546875
Outputs:
- grad_half: bfloat16 [4, 32, 8, 512], P('chan', 'grp')
- taps_grad: float32 [3, 3, 3, 128, 128], P(None, None, None, 'grp', 'chan')
All inputs are finite; a program needn't handle non-finite values.
Results may differ from a plain program's by a relative error of at most 0.0058.
Values may be sent and summed in bfloat16 or wider, within the bound.
No kernel may reach another device: no remote copies, remote signals or barrier semaphores. Data moves between devices by JAX's collectives and lax.ppermute only.
A program may use at most 64 MiB of HBM per device.

v0:
```python
import jax
import jax.numpy as jnp
from jax import lax
from jax.sharding import PartitionSpec as P


def padded_2(cells, sides, width):
    for axis, dim in sides:
        count = lax.axis_size(axis)
        ends = count - 1
        head = lax.slice_in_dim(cells, 0, width, axis=dim)
        tail = lax.slice_in_dim(cells, cells.shape[dim] - width, cells.shape[dim], axis=dim)
        cells = jnp.concatenate(
            [
                lax.ppermute(tail, axis, [(i, (i + 1) % count) for i in range(ends)]),
                cells,
                lax.ppermute(head, axis, [((i + 1) % count, i) for i in range(ends)]),
            ],
            axis=dim,
        )
    return cells


def spread_taps(padded, weight, extent, summed, swapped):
    for p in range(3):
        for q in range(3):
            for r in range(3):
                window = padded[
                    2 - p : 2 - p + extent[0], 2 - q : 2 - q + extent[1], 2 - r : 2 - r + extent[2]
                ]
                kernel = weight[q, p, r] if swapped else weight[p, q, r]
                summed = summed + jnp.einsum(
                    "xyzo,io->xyzi", window, kernel, preferred_element_type=jnp.float32
                )
    return summed


def body(grad_out, feat_full, filters_full, upsample_weight, filters_half):
    extent = grad_out.shape[:3]
    channels = grad_out.shape[3]
    stacked = jnp.stack([grad_out, feat_full])
    bordered = padded_2(stacked, (("grp", 1), ("chan", 2)), 1)
    bordered = jnp.pad(bordered, ((0, 0), (0, 0), (0, 0), (1, 1), (0, 0)))
    zeroed = jnp.zeros(extent + (channels,), jnp.float32)
    input_grad = spread_taps(bordered[0], filters_full, extent, zeroed, False).astype(jnp.bfloat16)
    features = bordered[1]
    tap_list = []
    for p in range(3):
        for q in range(3):
            for r in range(3):
                window = features[p : p + extent[0], q : q + extent[1], r : r + extent[2]]
                tap_list.append(
                    jnp.einsum(
                        "xyzi,xyzo->io", window, grad_out, preferred_element_type=jnp.float32
                    )
                )
    partial_taps = jnp.stack(tap_list).reshape(3, 3, 3, channels, channels)
    across = lax.psum_scatter(partial_taps, "grp", scatter_dimension=3, tiled=True)
    taps_grad = lax.psum_scatter(across, "chan", scatter_dimension=4, tiled=True)
    halves = input_grad.reshape(extent[0] // 2, 2, extent[1] // 2, 2, extent[2] // 2, 2, channels)
    coarse = jnp.einsum(
        "iajbkcd,abced->jike", halves, upsample_weight, preferred_element_type=jnp.float32
    ).astype(jnp.bfloat16)
    coarse_extent = coarse.shape[:3]
    wide = filters_half.shape[3]
    slab = lax.all_to_all(coarse, "chan", split_axis=3, concat_axis=0, tiled=True)
    slab = padded_2(slab, (("grp", 1),), 1)
    slab = jnp.pad(slab, ((1, 1), (0, 0), (1, 1), (0, 0)))
    count = lax.axis_size("chan") * coarse_extent[0]
    blank = jnp.zeros((count, coarse_extent[1], coarse_extent[2], wide), jnp.float32)
    result = lax.psum_scatter(
        spread_taps(slab, filters_half, (count, coarse_extent[1], coarse_extent[2]), blank, True),
        "chan",
        scatter_dimension=0,
        tiled=True,
    )
    grad_half = result.astype(jnp.bfloat16)
    return (grad_half, taps_grad)


def solution(mesh):
    in_specs = (
        P("grp", "chan", None, None),
        P("grp", "chan", None, None),
        P(),
        P(),
        P(None, None, None, None, "chan"),
    )
    out_specs = (P("chan", "grp", None, None), P(None, None, None, "grp", "chan"))
    return jax.shard_map(body, mesh=mesh, in_specs=in_specs, out_specs=out_specs, check_vma=False)
```

profile of v0, /device:TPU:0, one launch (start us, length us, event | category | flops | bytes accessed | tf_op | source)
XLA Modules:
  0.0 166.8 jit_solution(15116668181056318444)
XLA Ops:
  8.1 4.9 %collective-permute-start = (bf16[2,1,2,16,128]{4,3,2,1,0:T(8,128)(2,1)S(1)}, bf16[2,1,2,16,128]{4,3,2,1,0:T(8,128)(2,1)S(1)}, u32[]{:S(2)}, u32[]{:S(2)}) collective-permute-start(bf16[2,1,2,16,128]{4,3,2,1,0:T(8,128)(2,1)S(1)} %get-tuple-element.6), channel_id=1, source_target_pairs={{0,4},{4,8},{8,12},{12,16},{16,20},{20,24},{24,28},{1,5},{5,9},{9,... | collective-permute-start | bytes 49160 | tf_op jit(solution)/shard_map/ppermute | solution.py:15
  13.0 1.3 collective-permute-start.1
  14.4 4.2 %collective-permute-done.1 = bf16[2,1,2,16,128]{4,3,2,1,0:T(8,128)(2,1)S(1)} collective-permute-done((bf16[2,1,2,16,128]{4,3,2,1,0:T(8,128)(2,1)S(1)}, bf16[2,1,2,16,128]{4,3,2,1,0:T(8,128)(2,1)S(1)}, u32[]{:S(2)}, u32[]{:S(2)}) %collective-permute-start.1) | collective-permute-done | bytes 16416 | tf_op jit(solution)/shard_map/ppermute | solution.py:17
  19.5 1.3 collective-permute-start.2
  20.8 1.3 collective-permute-start.3
  22.1 3.6 %collective-permute-done.3 = bf16[2,10,1,16,128]{4,3,2,1,0:T(8,128)(2,1)S(1)} collective-permute-done((bf16[2,10,1,16,128]{4,3,2,1,0:T(8,128)(2,1)S(1)}, bf16[2,10,1,16,128]{4,3,2,1,0:T(8,128)(2,1)S(1)}, u32[]{:S(2)}, u32[]{:S(2)}) %collective-permute-start.3) | collective-permute-done | bytes 81952 | tf_op jit(solution)/shard_map/ppermute | solution.py:17
  25.7 1.1 select_maximum_fusion
  32.2 1.1 reshape.101
  33.3 4.4 %all-to-all-start = ((bf16[4,2,2048]{2,1,0:T(2,128)(2,1)}), bf16[4,2,2048]{2,1,0:T(2,128)(2,1)S(1)}, u32[]{:S(2)}, u32[]{:S(2)}) async-start(bf16[4,2,2048]{2,1,0:T(2,128)(2,1)} %reshape.101), calls=%async_computation | async-start | bytes 65536 | tf_op jit(solution)/shard_map/all_to_all | solution.py:66
  43.2 1.2 copy-done.2
  45.4 4.3 %collective-permute-start.4 = (bf16[4,1,8,128]{3,2,1,0:T(8,128)(2,1)S(1)}, bf16[4,1,8,128]{3,2,1,0:T(8,128)(2,1)S(1)}, u32[]{:S(2)}, u32[]{:S(2)}) collective-permute-start(bf16[4,1,8,128]{3,2,1,0:T(8,128)(2,1)S(1)} %get-tuple-element.8), channel_id=1, source_target_pairs={{0,4},{4,8},{8,12},{12,16},{16,20},{20,24},{24,28},{1,5},{5,9},{9,... | collective-permute-start | bytes 24584 | tf_op jit(solution)/shard_map/ppermute | solution.py:15
  49.7 1.6 collective-permute-start.5
  52.4 3.1 %collective-permute-done.5 = bf16[4,1,8,128]{3,2,1,0:T(8,128)(2,1)S(1)} collective-permute-done((bf16[4,1,8,128]{3,2,1,0:T(8,128)(2,1)S(1)}, bf16[4,1,8,128]{3,2,1,0:T(8,128)(2,1)S(1)}, u32[]{:S(2)}, u32[]{:S(2)}) %collective-permute-start.5) | collective-permute-done | bytes 8224 | tf_op jit(solution)/shard_map/ppermute | solution.py:17
  55.6 1.1 fusion.59
  58.9 1.1 fusion.65
  60.0 1.1 fusion.69
  62.2 1.1 fusion.87
  67.9 46.4 %reduce-scatter.8.cloned.1.call-done = f32[3,3,3,16,128]{4,3,2,1,0:T(8,128)} async-done(((f32[3,3,3,128,128]{4,3,2,1,0:T(8,128)}), f32[3,3,3,16,128]{4,3,2,1,0:T(8,128)}) %reduce-scatter.8.cloned.1.call-update) | async-done | bytes 221200 | tf_op jit(solution)/shard_map/reduce_scatter | solution.py:58
  114.3 2.5 %copy.99 = f32[3,3,3,16,128]{3,2,1,0,4:T(4,128)S(1)} copy(f32[3,3,3,16,128]{4,3,2,1,0:T(8,128)} %reduce-scatter.8.cloned.1.call-done) | data formatting | bytes 442368
  116.8 1.7 %reshape.99 = f32[128,432]{1,0:T(8,128)} reshape(f32[128,3,3,3,16]{4,3,2,1,0:T(4,128)S(1)} %bitcast.656) | data formatting | bytes 442368
  118.5 17.2 %reduce-scatter.6.cloned.1.call-done = f32[1,4,8,512]{3,2,1,0:T(8,128)} async-done(((f32[4,4,8,512]{3,2,1,0:T(8,128)}), f32[1,4,8,512]{3,2,1,0:T(8,128)}) %reduce-scatter.6.cloned.1.call-update) | async-done | bytes 65552 | tf_op jit(solution)/shard_map/reduce_scatter | solution.py:71
  135.7 1.5 convert_element_type.27
  137.2 21.1 %reduce-scatter.10.cloned.1.call-done = f32[32,432]{1,0:T(8,128)} async-done(((f32[128,432]{1,0:T(8,128)}), f32[32,432]{1,0:T(8,128)}) %reduce-scatter.10.cloned.1.call-update) | async-done | bytes 55312
  158.3 1.1 reshape.100
  (107 shorter events, 23.2 us)
Async XLA Ops:
  7.2 24.3 %copy-start = (bf16[2,2,2,512,128]{4,3,2,1,0:T(8,128)(2,1)S(1)}, bf16[2,2,2,512,128]{4,3,2,1,0:T(8,128)(2,1)}, u32[]{:S(2)}) copy-start(bf16[2,2,2,512,128]{4,3,2,1,0:T(8,128)(2,1)} %param.8) | copy-start | bytes 3145732
  7.2 19.7 %copy-start.3 = (bf16[3,3,3,128,128]{4,3,2,1,0:T(8,128)(2,1)S(1)}, bf16[3,3,3,128,128]{4,3,2,1,0:T(8,128)(2,1)}, u32[]{:S(2)}) copy-start(bf16[3,3,3,128,128]{4,3,2,1,0:T(8,128)(2,1)} %param.7) | copy-start | bytes 2654212
  8.1 6.3 %collective-permute-start = (bf16[2,1,2,16,128]{4,3,2,1,0:T(8,128)(2,1)S(1)}, bf16[2,1,2,16,128]{4,3,2,1,0:T(8,128)(2,1)S(1)}, u32[]{:S(2)}, u32[]{:S(2)}) collective-permute-start(bf16[2,1,2,16,128]{4,3,2,1,0:T(8,128)(2,1)S(1)} %get-tuple-element.6), channel_id=1, source_target_pairs={{0,4},{4,8},{8,12},{12,16},{16,20},{20,24},{24,28},{1,5},{5,9},{9,... | collective-permute-start | bytes 49160 | tf_op jit(solution)/shard_map/ppermute | solution.py:15
  13.0 5.6 %collective-permute-start.1 = (bf16[2,1,2,16,128]{4,3,2,1,0:T(8,128)(2,1)S(1)}, bf16[2,1,2,16,128]{4,3,2,1,0:T(8,128)(2,1)S(1)}, u32[]{:S(2)}, u32[]{:S(2)}) collective-permute-start(bf16[2,1,2,16,128]{4,3,2,1,0:T(8,128)(2,1)S(1)} %get-tuple-element.7), channel_id=1, source_target_pairs={{4,0},{8,4},{12,8},{16,12},{20,16},{24,20},{28,24},{5,1},{9,5},{13... | collective-permute-start | bytes 49160 | tf_op jit(solution)/shard_map/ppermute | solution.py:17
  19.5 2.6 %collective-permute-start.2 = (bf16[2,10,1,16,128]{4,3,2,1,0:T(8,128)(2,1)S(1)}, bf16[2,10,1,16,128]{4,3,2,1,0:T(8,128)(2,1)S(1)}, u32[]{:S(2)}, u32[]{:S(2)}) collective-permute-start(bf16[2,10,1,16,128]{4,3,2,1,0:T(8,128)(2,1)S(1)} %get-tuple-element.4), channel_id=1, source_target_pairs={{0,1},{1,2},{2,3},{4,5},{5,6},{6,7},{8,9},{9,10},{10,11},{12,13},{... | collective-permute-start | bytes 245768 | tf_op jit(solution)/shard_map/ppermute | solution.py:15
  20.8 4.9 %collective-permute-start.3 = (bf16[2,10,1,16,128]{4,3,2,1,0:T(8,128)(2,1)S(1)}, bf16[2,10,1,16,128]{4,3,2,1,0:T(8,128)(2,1)S(1)}, u32[]{:S(2)}, u32[]{:S(2)}) collective-permute-start(bf16[2,10,1,16,128]{4,3,2,1,0:T(8,128)(2,1)S(1)} %get-tuple-element.5), channel_id=1, source_target_pairs={{1,0},{2,1},{3,2},{5,4},{6,5},{7,6},{9,8},{10,9},{11,10},{13,12},{... | collective-permute-start | bytes 245768 | tf_op jit(solution)/shard_map/ppermute | solution.py:17
  31.3 6.4 %copy-start.4 = (bf16[8,2,16,128]{3,2,1,0:T(8,128)(2,1)S(1)}, bf16[8,2,16,128]{3,2,1,0:T(8,128)(2,1)}, u32[]{:S(2)}) copy-start(bf16[8,2,16,128]{3,2,1,0:T(8,128)(2,1)} %param.5) | copy-start | bytes 196612
  33.3 11.2 %all-to-all-start = ((bf16[4,2,2048]{2,1,0:T(2,128)(2,1)}), bf16[4,2,2048]{2,1,0:T(2,128)(2,1)S(1)}, u32[]{:S(2)}, u32[]{:S(2)}) async-start(bf16[4,2,2048]{2,1,0:T(2,128)(2,1)} %reshape.101), calls=%async_computation | async-start | bytes 65536 | tf_op jit(solution)/shard_map/all_to_all | solution.py:66
  37.7 76.6 %reduce-scatter.8.cloned.1.call-start = ((), (), s32[]{:S(2)}) async-start(), calls=%async_computation.5 | async-start | bytes 1990656 | tf_op jit(solution)/shard_map/reduce_scatter | solution.py:58
  43.2 1.3 copy-start.2
  44.5 91.3 %reduce-scatter.6.cloned.1.call-start = ((), (), s32[]{:S(2)}) async-start(), calls=%async_computation.4 | async-start | bytes 327680 | tf_op jit(solution)/shard_map/reduce_scatter | solution.py:71
  45.4 7.0 %collective-permute-start.4 = (bf16[4,1,8,128]{3,2,1,0:T(8,128)(2,1)S(1)}, bf16[4,1,8,128]{3,2,1,0:T(8,128)(2,1)S(1)}, u32[]{:S(2)}, u32[]{:S(2)}) collective-permute-start(bf16[4,1,8,128]{3,2,1,0:T(8,128)(2,1)S(1)} %get-tuple-element.8), channel_id=1, source_target_pairs={{0,4},{4,8},{8,12},{12,16},{16,20},{20,24},{24,28},{1,5},{5,9},{9,... | collective-permute-start | bytes 24584 | tf_op jit(solution)/shard_map/ppermute | solution.py:15
  49.7 13.6 %copy-start.1 = (bf16[3,3,3,512,128]{4,3,2,1,0:T(8,128)(2,1)S(1)}, bf16[3,3,3,512,128]{4,3,2,1,0:T(8,128)(2,1)}, u32[]{:S(2)}) copy-start(bf16[3,3,3,512,128]{4,3,2,1,0:T(8,128)(2,1)} %param.9) | copy-start | bytes 10616836
  49.7 5.8 %collective-permute-start.5 = (bf16[4,1,8,128]{3,2,1,0:T(8,128)(2,1)S(1)}, bf16[4,1,8,128]{3,2,1,0:T(8,128)(2,1)S(1)}, u32[]{:S(2)}, u32[]{:S(2)}) collective-permute-start(bf16[4,1,8,128]{3,2,1,0:T(8,128)(2,1)S(1)} %get-tuple-element.9), channel_id=1, source_target_pairs={{4,0},{8,4},{12,8},{16,12},{20,16},{24,20},{28,24},{5,1},{9,5},{13... | collective-permute-start | bytes 24584 | tf_op jit(solution)/shard_map/ppermute | solution.py:17
  67.9 90.4 %reduce-scatter.10.cloned.1.call-start = ((), (), s32[]{:S(2)}) async-start(), calls=%async_computation.6 | async-start | bytes 327680
Sparse Core Ops, SparseCore 0:
  44.6 69.6 reduce-scatter.7
  116.8 18.9 reduce-scatter.5
  138.2 20.0 reduce-scatter.9
where the time goes:
time: 168 us; the launch traced here: 167 us
  waiting for transfers between devices  95.8 us (57%)
  matrix products  23.3 us (14%)
  starting transfers between devices  19.1 us (11%)
  between operations  14.4 us (9%)
  local copies, waits for them, and re-layouts  9.76 us (6%)
  other arithmetic  4.41 us (3%)
    reduce_scatter x1, waiting for transfers between devices, body(): lax.psum_scatter(partial_taps, 'grp', scatter_dimension=3, tiled=True)  46.4 us
    unnamed x4, waiting for transfers between devices  21.2 us
    dot_general x54, matrix products, spread_taps(): jnp.einsum('xyzo,io->xyzi', window, kernel, preferred_element_type=jnp.fl...  17.5 us
    reduce_scatter x1, waiting for transfers between devices, body(): lax.psum_scatter(spread_taps(slab, filters_half, (count, coarse_extent[1]...  17.2 us
    ppermute x3, waiting for transfers between devices, padded_2(): lax.ppermute(head, axis, [((i + 1) % count, i) for i in range(ends)])  10.9 us
    ppermute x3, starting transfers between devices, padded_2(): lax.ppermute(tail, axis, [(i, (i + 1) % count) for i in range(ends)])  10.5 us
    unnamed x16, local copies, waits for them, and re-layouts  9.16 us
    dot_general x27, matrix products, body(): jnp.einsum('xyzi,xyzo->io', window, grad_out, preferred_element_type=jnp....  5.4 us
  transfers between devices with their start and end apart: 10, of which 7 were waited for; matrix products, arithmetic and copies ran while one was open for 15% of the time, Pallas kernels for 0%

commit v1 on v0

--- a/solution.py
+++ b/solution.py
@@ -1,7 +1,23 @@
+import functools
 import jax
 import jax.numpy as jnp
 from jax import lax
 from jax.sharding import PartitionSpec as P
+
+
+def group_load(mat, lane_axis):
+    return jnp.concatenate(
+        lax.all_to_all(
+            jnp.stack(jnp.split(mat, lax.axis_size(lane_axis), 3)),
+            concat_axis=0,
+            split_axis=0,
+            axis_name=lane_axis,
+        ),
+        0,
+    )
+
+
+launch_row_all = functools.partial(group_load, lane_axis="chan")
 
 
 def padded_2(cells, sides, width):
@@ -63,7 +79,7 @@
     ).astype(jnp.bfloat16)
     coarse_extent = coarse.shape[:3]
     wide = filters_half.shape[3]
-    slab = lax.all_to_all(coarse, "chan", split_axis=3, concat_axis=0, tiled=True)
+    slab = launch_row_all(coarse)
     slab = padded_2(slab, (("grp", 1),), 1)
     slab = jnp.pad(slab, ((1, 1), (0, 0), (1, 1), (0, 0)))
     count = lax.axis_size("chan") * coarse_extent[0]

time: 168 us -> 167 us (level)
  local copies, waits for them, and re-layouts: 9.76 us -> 7.51 us
    unnamed x16 -> x14, local copies, waits for them, and re-layouts: 9.16 us -> 7.43 us
where the time goes in v1:
time: 167 us; the launch traced here: 166 us
  waiting for transfers between devices  96.6 us (58%)
  matrix products  23.4 us (14%)
  starting transfers between devices  19.1 us (11%)
  between operations  14.4 us (9%)
  local copies, waits for them, and re-layouts  7.51 us (4%)
  other arithmetic  5.03 us (3%)
    reduce_scatter x1, waiting for transfers between devices, body(): lax.psum_scatter(partial_taps, 'grp', scatter_dimension=3, tiled=True)  47.1 us
    unnamed x4, waiting for transfers between devices  21.2 us
    dot_general x54, matrix products, spread_taps(): jnp.einsum('xyzo,io->xyzi', window, kernel, preferred_element_type=jnp.fl...  17.6 us
    reduce_scatter x1, waiting for transfers between devices, body(): lax.psum_scatter(spread_taps(slab, filters_half, (count, coarse_extent[1]...  17.2 us
    ppermute x3, waiting for transfers between devices, padded_2(): lax.ppermute(head, axis, [((i + 1) % count, i) for i in range(ends)])  10.9 us
    ppermute x3, starting transfers between devices, padded_2(): lax.ppermute(tail, axis, [(i, (i + 1) % count) for i in range(ends)])  10.5 us
    unnamed x14, local copies, waits for them, and re-layouts  7.43 us
    dot_general x27, matrix products, body(): jnp.einsum('xyzi,xyzo->io', window, grad_out, preferred_element_type=jnp....  5.4 us
  transfers between devices with their start and end apart: 10, of which 7 were waited for; matrix products, arithmetic and copies ran while one was open for 15% of the time, Pallas kernels for 0%

profile of v1, /device:TPU:0, one launch (start us, length us, event | category | flops | bytes accessed | tf_op | source)
XLA Modules:
  0.0 166.0 jit_solution(7691122758829953899)
XLA Ops:
  8.1 4.9 %collective-permute-start = (bf16[2,1,2,16,128]{4,3,2,1,0:T(8,128)(2,1)S(1)}, bf16[2,1,2,16,128]{4,3,2,1,0:T(8,128)(2,1)S(1)}, u32[]{:S(2)}, u32[]{:S(2)}) collective-permute-start(bf16[2,1,2,16,128]{4,3,2,1,0:T(8,128)(2,1)S(1)} %get-tuple-element.6), channel_id=1, source_target_pairs={{0,4},{4,8},{8,12},{12,16},{16,20},{20,24},{24,28},{1,5},{5,9},{9,... | collective-permute-start | bytes 49160 | tf_op jit(solution)/shard_map/ppermute | solution.py:31
  13.0 1.3 collective-permute-start.1
  14.4 4.2 %collective-permute-done.1 = bf16[2,1,2,16,128]{4,3,2,1,0:T(8,128)(2,1)S(1)} collective-permute-done((bf16[2,1,2,16,128]{4,3,2,1,0:T(8,128)(2,1)S(1)}, bf16[2,1,2,16,128]{4,3,2,1,0:T(8,128)(2,1)S(1)}, u32[]{:S(2)}, u32[]{:S(2)}) %collective-permute-start.1) | collective-permute-done | bytes 16416 | tf_op jit(solution)/shard_map/ppermute | solution.py:33
  19.5 1.3 collective-permute-start.2
  20.8 1.3 collective-permute-start.3
  22.1 3.6 %collective-permute-done.3 = bf16[2,10,1,16,128]{4,3,2,1,0:T(8,128)(2,1)S(1)} collective-permute-done((bf16[2,10,1,16,128]{4,3,2,1,0:T(8,128)(2,1)S(1)}, bf16[2,10,1,16,128]{4,3,2,1,0:T(8,128)(2,1)S(1)}, u32[]{:S(2)}, u32[]{:S(2)}) %collective-permute-start.3) | collective-permute-done | bytes 81952 | tf_op jit(solution)/shard_map/ppermute | solution.py:33
  25.7 1.1 select_maximum_fusion
  32.6 4.4 %all-to-all-start = ((bf16[4,1,4,8,128]{4,3,2,1,0:T(8,128)(2,1)}), bf16[4,1,4,8,128]{4,3,2,1,0:T(8,128)(2,1)S(1)}, u32[]{:S(2)}, u32[]{:S(2)}) async-start(bf16[4,1,4,8,128]{4,3,2,1,0:T(8,128)(2,1)} %pad_maximum_fusion.1), calls=%async_computation | async-start | bytes 65536 | tf_op jit(solution)/shard_map/all_to_all | solution.py:10
  42.4 1.2 copy-done.2
  43.7 4.3 %collective-permute-start.4 = (bf16[4,1,8,128]{3,2,1,0:T(8,128)(2,1)S(1)}, bf16[4,1,8,128]{3,2,1,0:T(8,128)(2,1)S(1)}, u32[]{:S(2)}, u32[]{:S(2)}) collective-permute-start(bf16[4,1,8,128]{3,2,1,0:T(8,128)(2,1)S(1)} %get-tuple-element.8), channel_id=1, source_target_pairs={{0,4},{4,8},{8,12},{12,16},{16,20},{20,24},{24,28},{1,5},{5,9},{9,... | collective-permute-start | bytes 24584 | tf_op jit(solution)/shard_map/ppermute | solution.py:31
  48.1 1.6 collective-permute-start.5
  50.8 3.1 %collective-permute-done.5 = bf16[4,1,8,128]{3,2,1,0:T(8,128)(2,1)S(1)} collective-permute-done((bf16[4,1,8,128]{3,2,1,0:T(8,128)(2,1)S(1)}, bf16[4,1,8,128]{3,2,1,0:T(8,128)(2,1)S(1)}, u32[]{:S(2)}, u32[]{:S(2)}) %collective-permute-start.5) | collective-permute-done | bytes 8224 | tf_op jit(solution)/shard_map/ppermute | solution.py:33
  54.0 1.1 fusion.59
  55.1 1.1 fusion.61
  57.3 1.1 fusion.65
  58.4 1.1 fusion.69
  59.5 1.1 fusion.73
  66.3 47.1 %reduce-scatter.8.cloned.1.call-done = f32[3,3,3,16,128]{4,3,2,1,0:T(8,128)} async-done(((f32[3,3,3,128,128]{4,3,2,1,0:T(8,128)}), f32[3,3,3,16,128]{4,3,2,1,0:T(8,128)}) %reduce-scatter.8.cloned.1.call-update) | async-done | bytes 221200 | tf_op jit(solution)/shard_map/reduce_scatter | solution.py:74
  113.4 2.5 %copy.91 = f32[3,3,3,16,128]{3,2,1,0,4:T(4,128)S(1)} copy(f32[3,3,3,16,128]{4,3,2,1,0:T(8,128)} %reduce-scatter.8.cloned.1.call-done) | data formatting | bytes 442368
  115.9 1.7 %reshape.103 = f32[128,432]{1,0:T(8,128)} reshape(f32[128,3,3,3,16]{4,3,2,1,0:T(4,128)S(1)} %bitcast.659) | data formatting | bytes 442368
  117.6 17.2 %reduce-scatter.6.cloned.1.call-done = f32[1,4,8,512]{3,2,1,0:T(8,128)} async-done(((f32[4,4,8,512]{3,2,1,0:T(8,128)}), f32[1,4,8,512]{3,2,1,0:T(8,128)}) %reduce-scatter.6.cloned.1.call-update) | async-done | bytes 65552 | tf_op jit(solution)/shard_map/reduce_scatter | solution.py:87
  134.9 1.5 convert_element_type.27
  136.3 21.1 %reduce-scatter.10.cloned.1.call-done = f32[32,432]{1,0:T(8,128)} async-done(((f32[128,432]{1,0:T(8,128)}), f32[32,432]{1,0:T(8,128)}) %reduce-scatter.10.cloned.1.call-update) | async-done | bytes 55312
  157.4 1.1 reshape.104
  (105 shorter events, 21.6 us)
Async XLA Ops:
  7.2 24.3 %copy-start = (bf16[2,2,2,512,128]{4,3,2,1,0:T(8,128)(2,1)S(1)}, bf16[2,2,2,512,128]{4,3,2,1,0:T(8,128)(2,1)}, u32[]{:S(2)}) copy-start(bf16[2,2,2,512,128]{4,3,2,1,0:T(8,128)(2,1)} %param.8) | copy-start | bytes 3145732
  7.2 19.7 %copy-start.3 = (bf16[3,3,3,128,128]{4,3,2,1,0:T(8,128)(2,1)S(1)}, bf16[3,3,3,128,128]{4,3,2,1,0:T(8,128)(2,1)}, u32[]{:S(2)}) copy-start(bf16[3,3,3,128,128]{4,3,2,1,0:T(8,128)(2,1)} %param.7) | copy-start | bytes 2654212
  8.1 6.3 %collective-permute-start = (bf16[2,1,2,16,128]{4,3,2,1,0:T(8,128)(2,1)S(1)}, bf16[2,1,2,16,128]{4,3,2,1,0:T(8,128)(2,1)S(1)}, u32[]{:S(2)}, u32[]{:S(2)}) collective-permute-start(bf16[2,1,2,16,128]{4,3,2,1,0:T(8,128)(2,1)S(1)} %get-tuple-element.6), channel_id=1, source_target_pairs={{0,4},{4,8},{8,12},{12,16},{16,20},{20,24},{24,28},{1,5},{5,9},{9,... | collective-permute-start | bytes 49160 | tf_op jit(solution)/shard_map/ppermute | solution.py:31
  13.0 5.6 %collective-permute-start.1 = (bf16[2,1,2,16,128]{4,3,2,1,0:T(8,128)(2,1)S(1)}, bf16[2,1,2,16,128]{4,3,2,1,0:T(8,128)(2,1)S(1)}, u32[]{:S(2)}, u32[]{:S(2)}) collective-permute-start(bf16[2,1,2,16,128]{4,3,2,1,0:T(8,128)(2,1)S(1)} %get-tuple-element.7), channel_id=1, source_target_pairs={{4,0},{8,4},{12,8},{16,12},{20,16},{24,20},{28,24},{5,1},{9,5},{13... | collective-permute-start | bytes 49160 | tf_op jit(solution)/shard_map/ppermute | solution.py:33
  19.5 2.6 %collective-permute-start.2 = (bf16[2,10,1,16,128]{4,3,2,1,0:T(8,128)(2,1)S(1)}, bf16[2,10,1,16,128]{4,3,2,1,0:T(8,128)(2,1)S(1)}, u32[]{:S(2)}, u32[]{:S(2)}) collective-permute-start(bf16[2,10,1,16,128]{4,3,2,1,0:T(8,128)(2,1)S(1)} %get-tuple-element.4), channel_id=1, source_target_pairs={{0,1},{1,2},{2,3},{4,5},{5,6},{6,7},{8,9},{9,10},{10,11},{12,13},{... | collective-permute-start | bytes 245768 | tf_op jit(solution)/shard_map/ppermute | solution.py:31
  20.8 4.9 %collective-permute-start.3 = (bf16[2,10,1,16,128]{4,3,2,1,0:T(8,128)(2,1)S(1)}, bf16[2,10,1,16,128]{4,3,2,1,0:T(8,128)(2,1)S(1)}, u32[]{:S(2)}, u32[]{:S(2)}) collective-permute-start(bf16[2,10,1,16,128]{4,3,2,1,0:T(8,128)(2,1)S(1)} %get-tuple-element.5), channel_id=1, source_target_pairs={{1,0},{2,1},{3,2},{5,4},{6,5},{7,6},{9,8},{10,9},{11,10},{13,12},{... | collective-permute-start | bytes 245768 | tf_op jit(solution)/shard_map/ppermute | solution.py:33
  30.8 6.1 %copy-start.4 = (bf16[8,2,16,128]{3,2,1,0:T(8,128)(2,1)S(1)}, bf16[8,2,16,128]{3,2,1,0:T(8,128)(2,1)}, u32[]{:S(2)}) copy-start(bf16[8,2,16,128]{3,2,1,0:T(8,128)(2,1)} %param.5) | copy-start | bytes 196612
  32.6 11.2 %all-to-all-start = ((bf16[4,1,4,8,128]{4,3,2,1,0:T(8,128)(2,1)}), bf16[4,1,4,8,128]{4,3,2,1,0:T(8,128)(2,1)S(1)}, u32[]{:S(2)}, u32[]{:S(2)}) async-start(bf16[4,1,4,8,128]{4,3,2,1,0:T(8,128)(2,1)} %pad_maximum_fusion.1), calls=%async_computation | async-start | bytes 65536 | tf_op jit(solution)/shard_map/all_to_all | solution.py:10
  36.9 76.5 %reduce-scatter.8.cloned.1.call-start = ((), (), s32[]{:S(2)}) async-start(), calls=%async_computation.5 | async-start | bytes 1990656 | tf_op jit(solution)/shard_map/reduce_scatter | solution.py:74
  42.4 1.2 copy-start.2
  43.7 91.2 %reduce-scatter.6.cloned.1.call-start = ((), (), s32[]{:S(2)}) async-start(), calls=%async_computation.4 | async-start | bytes 327680 | tf_op jit(solution)/shard_map/reduce_scatter | solution.py:87
  43.7 7.0 %collective-permute-start.4 = (bf16[4,1,8,128]{3,2,1,0:T(8,128)(2,1)S(1)}, bf16[4,1,8,128]{3,2,1,0:T(8,128)(2,1)S(1)}, u32[]{:S(2)}, u32[]{:S(2)}) collective-permute-start(bf16[4,1,8,128]{3,2,1,0:T(8,128)(2,1)S(1)} %get-tuple-element.8), channel_id=1, source_target_pairs={{0,4},{4,8},{8,12},{12,16},{16,20},{20,24},{24,28},{1,5},{5,9},{9,... | collective-permute-start | bytes 24584 | tf_op jit(solution)/shard_map/ppermute | solution.py:31
  48.1 13.6 %copy-start.1 = (bf16[3,3,3,512,128]{4,3,2,1,0:T(8,128)(2,1)S(1)}, bf16[3,3,3,512,128]{4,3,2,1,0:T(8,128)(2,1)}, u32[]{:S(2)}) copy-start(bf16[3,3,3,512,128]{4,3,2,1,0:T(8,128)(2,1)} %param.9) | copy-start | bytes 10616836
  48.1 5.8 %collective-permute-start.5 = (bf16[4,1,8,128]{3,2,1,0:T(8,128)(2,1)S(1)}, bf16[4,1,8,128]{3,2,1,0:T(8,128)(2,1)S(1)}, u32[]{:S(2)}, u32[]{:S(2)}) collective-permute-start(bf16[4,1,8,128]{3,2,1,0:T(8,128)(2,1)S(1)} %get-tuple-element.9), channel_id=1, source_target_pairs={{4,0},{8,4},{12,8},{16,12},{20,16},{24,20},{28,24},{5,1},{9,5},{13... | collective-permute-start | bytes 24584 | tf_op jit(solution)/shard_map/ppermute | solution.py:33
  66.2 91.2 %reduce-scatter.10.cloned.1.call-start = ((), (), s32[]{:S(2)}) async-start(), calls=%async_computation.6 | async-start | bytes 327680
Sparse Core Ops, SparseCore 0:
  43.8 69.5 reduce-scatter.7
  115.9 18.9 reduce-scatter.5
  137.3 20.0 reduce-scatter.9
